TPU v7x, 512 devices: a whole 4x4x16 slice. The times are simulated.
512 devices in a mesh: tiles: 128 (over z, y, core), rep: 4 (over x).
Axes of the slice: x: 4, y: 4, z: 16, core: 2. Of those that a mesh axis runs over, the one named last changes fastest.
Arguments:
- tiles: bfloat16 [1024, 64, 4096], P(('tiles', 'rep')), may hold values from -6 to 6
- block_one: int32 [1024], P(('tiles', 'rep')), may hold values from 0 to 127
- block_two: int32 [1024], P(('tiles', 'rep')), may hold values from 0 to 255
- block_three: int32 [1024], P(('tiles', 'rep')), may hold values from 0 to 15
- owner_map: int32 [128], replicated, may hold values from 0 to 127, each once
- u_one: float32 [32, 8192], P(None, 'tiles'), may hold values from -6 to 6
- u_two: bfloat16 [32, 16384], P(None, 'tiles'), may hold values from -6 to 6
- u_three: bfloat16 [32, 1024], replicated, may hold values from -6 to 6
Outputs:
- factor: float32 [32, 8192], P(None, 'tiles')
- tile_factor: bfloat16 [1024, 2048], P(('tiles', 'rep'))
All inputs are finite; a program needn't handle non-finite values.
Results may differ from a plain program's by a relative error of at most 0.0081.
Values may be sent and summed in bfloat16 or wider, within the bound.
A program may use at most 64 MiB of HBM per device.

v0:
```python
import jax
import jax.numpy as jnp
from jax import lax
from jax.sharding import PartitionSpec as P

NS_STEPS = 2


def pick(table, index, width):
    grid = table.reshape(table.shape[0], -1, width)
    return jnp.transpose(jnp.take(grid, index, axis=1), (1, 0, 2))


def gram_total(local):
    return lax.psum(local, "tiles")


def orthonormal(rows, rows_total):
    hi = lax.Precision.HIGHEST
    rank = rows.shape[0]
    g0 = gram_total(jnp.dot(rows, rows.T, precision=hi, preferred_element_type=jnp.float32))
    msq = jnp.trace(g0) / rows_total
    inv = 1.0 / jnp.sqrt(msq + 1e-06)
    x = rows * inv
    g = g0 * (inv * inv) / rows_total
    eye = jnp.eye(rank, dtype=jnp.float32)
    for step in range(NS_STEPS):
        if step > 0:
            g = (
                gram_total(jnp.dot(x, x.T, precision=hi, preferred_element_type=jnp.float32))
                / rows_total
            )
        x = jnp.dot(1.5 * eye - 0.5 * g, x, precision=hi, preferred_element_type=jnp.float32)
    return x


def spread(current):
    cast = current.astype(jnp.bfloat16)
    return lax.all_gather(cast, "tiles", axis=1, tiled=True)


def per_device(tiles, block_one, block_two, block_three, owner_map, u_one, u_two, u_three):
    hi = lax.Precision.HIGHEST
    count = tiles.shape[0]
    width = tiles.shape[1]
    rank = u_three.shape[0]
    blocks_total = owner_map.shape[0]
    rows_total = blocks_total * width
    two_full = lax.all_gather(u_two, "tiles", axis=1, tiled=True)
    two_pick = pick(two_full, block_two, width)
    three_pick = pick(u_three, block_three, width)
    cube = tiles.reshape(count, width, width, width)
    first = jnp.einsum(
        "tijk,tsk->tijs", cube, three_pick, preferred_element_type=jnp.float32
    ).astype(jnp.bfloat16)
    second = jnp.einsum("tijs,trj->tirs", first, two_pick, preferred_element_type=jnp.float32)
    products = second.reshape(count, width, rank * rank).astype(jnp.bfloat16)
    positions = jnp.take(owner_map, block_one)
    onehot = (positions[:, None] == jnp.arange(blocks_total, dtype=jnp.int32)[None, :]).astype(
        jnp.float32
    )
    current = u_one
    readers = pick(spread(current), positions, width)
    partial_value = jnp.einsum("tic,tri->rc", products, readers, preferred_element_type=jnp.float32)
    project = lax.psum(partial_value, ("tiles", "rep")).astype(jnp.bfloat16)
    z_tile = jnp.einsum("rc,tic->tri", project, products, preferred_element_type=jnp.float32)
    term = jnp.einsum("tri,tn->rni", z_tile, onehot, precision=hi).reshape(rank, rows_total)
    rows = lax.psum_scatter(term, "tiles", scatter_dimension=1, tiled=True)
    rows = lax.psum(rows, "rep")
    current = orthonormal(rows, rows_total)
    tile_factor = pick(spread(current), positions, width).reshape(count, rank * width)
    return (current, tile_factor)


def solution(mesh):
    in_specs = (
        P(("tiles", "rep"), None, None),
        P(("tiles", "rep")),
        P(("tiles", "rep")),
        P(("tiles", "rep")),
        P(),
        P(None, "tiles"),
        P(None, "tiles"),
        P(),
    )
    out_specs = (P(None, "tiles"), P(("tiles", "rep"), None))
    return jax.shard_map(
        per_device, mesh=mesh, in_specs=in_specs, out_specs=out_specs, check_vma=False
    )
```

profile of v0, /device:TPU:1, one launch (start us, length us, event | category | flops | bytes accessed | tf_op | source)
XLA Modules:
  0.0 1633.5 jit_solution(5011610970250502089)
XLA Ops:
  7.2 0.0 copy-start
  7.2 0.0 all-gather.4.cloned.1.call-start
  7.2 0.7 all-gather.4.cloned.1.call-update
  7.9 0.0 reduce-scatter.4.cloned.1.call-start
  8.0 0.7 compare_select_fusion.3
  8.6 0.7 convert_bitcast_fusion.1
  9.3 1.0 reshape.51
  10.4 109.1 %all-gather = bf16[128,64,32]{1,2,0:T(8,128)(2,1)S(1)} all-gather(bf16[1,64,32]{1,2,0:T(8,128)(2,1)S(1)} %convert_bitcast_fusion.1), channel_id=1, replica_groups=mesh['tiles'=128,'rep'=4] {'tiles'}, dimensions={0}, use_global_device_ids=true | all-gather | bytes 528384 | tf_op jit(solution)/shard_map/all_gather | solution.py:39
  119.5 0.4 copy.31
  119.9 0.8 reshape.103
  120.7 1.1 reshape.53
  121.9 0.7 copy.32
  122.6 3.4 reshape.52
  126.1 0.6 gather_fusion
  126.7 0.6 gather_fusion.2
  127.3 0.6 gather_fusion.3
  128.0 2.0 fusion
  130.0 17.5 %all-gather.4.cloned.1.call-done = bf16[32,16384]{1,0:T(8,128)(2,1)} async-done(((bf16[32,128]{1,0:T(8,128)(2,1)}), bf16[32,16384]{1,0:T(8,128)(2,1)}) %all-gather.4.cloned.1.call-update) | async-done | bytes 1048592 | tf_op jit(solution)/shard_map/all_gather | solution.py:49
  147.5 3.0 reshape.50
  150.6 2.7 copy.27
  153.3 2.1 gather_fusion.1
  155.4 1.1 fusion.1
  156.5 0.2 copy.30
  156.7 0.2 convolution_bitcast_fusion.1
  157.0 102.8 %all-reduce.1 = bf16[32,1024]{1,0:T(8,128)(2,1)S(1)} all-reduce(f32[32,1024]{1,0:T(8,128)S(1)} %convolution_bitcast_fusion.1), channel_id=1, replica_groups=mesh['tiles'=128,'rep'=4] {'tiles','rep'}, use_global_device_ids=true, to_apply=%region_0.0 | all-reduce | flops 32768 | bytes 196608 | tf_op jit(solution)/shard_map/psum | solution.py:65
  259.7 0.2 convolution_bitcast_fusion.2
  259.9 1.0 convolution_bitcast_fusion
  261.0 4.4 copy.45
  265.4 0.0 reduce-scatter.4.cloned.1.call-update
  265.5 245.9 %reduce-scatter.4.cloned.1.call-done = f32[64,32]{1,0:T(8,128)} async-done(((f32[8192,32]{1,0:T(8,128)}), f32[64,32]{1,0:T(8,128)}) %reduce-scatter.4.cloned.1.call-update) | async-done | bytes 8208
  511.3 0.8 copy.44
  512.2 13.3 psum.29
  525.5 0.1 fusion.44
  525.6 500.6 %psum.30 = f32[32,32]{1,0:T(8,128)S(1)} all-reduce(f32[32,32]{1,0:T(8,128)S(1)} %fusion.44), channel_id=1, replica_groups=mesh['tiles'=128,'rep'=4] {'tiles'}, use_global_device_ids=true, to_apply=%region_3.5 | all-reduce | flops 1024 | bytes 8192 | tf_op jit(solution)/shard_map/psum | solution.py:15
  1026.3 0.6 select_reduce_fusion
  1027.6 0.1 fusion.6
  1027.7 0.2 fusion.45
  1027.9 490.9 %psum.31 = f32[32,32]{1,0:T(8,128)S(1)} all-reduce(f32[32,32]{1,0:T(8,128)S(1)} %fusion.45), channel_id=1, replica_groups=mesh['tiles'=128,'rep'=4] {'tiles'}, use_global_device_ids=true, to_apply=%region_5.7 | all-reduce | flops 1024 | bytes 8192 | tf_op jit(solution)/shard_map/psum | solution.py:15
  1518.7 0.1 fusion.7
  1518.9 0.0 copy-start.1
  1518.9 103.3 %all-gather.1 = bf16[128,64,32]{1,2,0:T(8,128)(2,1)S(1)} all-gather(bf16[1,64,32]{1,2,0:T(8,128)(2,1)S(1)} %convert_bitcast_fusion), channel_id=1, replica_groups=mesh['tiles'=128,'rep'=4] {'tiles'}, dimensions={0}, use_global_device_ids=true | all-gather | bytes 528384 | tf_op jit(solution)/shard_map/all_gather | solution.py:39
  1622.2 0.4 copy.37
  1622.6 0.8 reshape.105
  1623.5 1.1 reshape.55
  1624.6 0.7 copy.38
  1625.3 0.6 gather_fusion.4
  1625.9 0.1 broadcast_select_fusion
  1625.9 0.7 reshape.56
  (20 shorter events, 0.1 us)
Async XLA Ops:
  7.2 118.9 %copy-start = (s32[128]{0:T(128)S(1)}, s32[128]{0:T(128)}, u32[]{:S(2)}) copy-start(s32[128]{0:T(128)} %param.14) | copy-start | bytes 1540
  7.2 140.3 %all-gather.4.cloned.1.call-start = ((), (), s32[]{:S(2)}) async-start(), calls=%async_computation.1 | async-start | bytes 1056768 | tf_op jit(solution)/shard_map/all_gather | solution.py:49
  7.9 503.4 %reduce-scatter.4.cloned.1.call-start = ((), (), s32[]{:S(2)}) async-start(), calls=%async_computation.2 | async-start | bytes 4227072
  122.6 4.2 copy-start.4
  122.6 4.7 copy-start.2
  122.6 5.3 copy-start.3
  1518.9 104.6 %copy-start.1 = (f32[32,64]{1,0:T(8,128)}, f32[32,64]{1,0:T(8,128)S(1)}, u32[]{:S(2)}) copy-start(f32[32,64]{1,0:T(8,128)S(1)} %fusion.7) | copy-start | bytes 24580
Sparse Core Ops, SparseCore 0:
  11.0 136.4 all-gather.3
  265.6 245.7 reduce-scatter.3
where the time goes:
time: 1630 us
  blocking collectives  1320 us (81%)
  waiting for transfers between devices  264 us (16%)
  local copies, waits for them, and re-layouts  27 us (2%)
    psum x2, blocking collectives, gram_total(): return lax.psum(local, 'tiles')  992 us
    unnamed x3, waiting for transfers between devices  247 us
    all_gather x2, blocking collectives, spread(): return lax.all_gather(cast, 'tiles', axis=1, tiled=True)  212 us
    psum x1, blocking collectives, per_device(): project = lax.psum(partial_value, ('tiles', 'rep')).astype(jnp.bfloat16)  103 us
  transfers between devices with their start and end apart: 2, of which 2 were waited for; matrix products, arithmetic and copies ran while one was open for 1% of the time, Pallas kernels for 0%

commit v1 on v0

--- a/solution.py
+++ b/solution.py
@@ -6,13 +6,18 @@
 NS_STEPS = 2
 
 
+def summed_here(block, axis):
+    parts = lax.all_gather(block, axis)
+    return jnp.sum(parts, axis=0)
+
+
 def pick(table, index, width):
     grid = table.reshape(table.shape[0], -1, width)
     return jnp.transpose(jnp.take(grid, index, axis=1), (1, 0, 2))
 
 
 def gram_total(local):
-    return lax.psum(local, "tiles")
+    return summed_here(local, "tiles")
 
 
 def orthonormal(rows, rows_total):

time: 1630 us -> 854 us (0.52)
  blocking collectives: 1320 us -> 540 us
    psum x2 -> x0, blocking collectives: 992 us -> none  [gram_total(): return lax.psum(local, 'tiles')]
    all_gather x0 -> x2, blocking collectives: none -> 215 us  [summed_here(): parts = lax.all_gather(block, axis)]
where the time goes in v1:
time: 854 us
  blocking collectives  540 us (63%)
  waiting for transfers between devices  264 us (31%)
  local copies, waits for them, and re-layouts  27 us (3%)
  between operations  15 us (2%)
    unnamed x3, waiting for transfers between devices  247 us
    all_gather x2, blocking collectives, summed_here(): parts = lax.all_gather(block, axis)  215 us
    all_gather x2, blocking collectives, spread(): return lax.all_gather(cast, 'tiles', axis=1, tiled=True)  209 us
    psum x1, blocking collectives, per_device(): project = lax.psum(partial_value, ('tiles', 'rep')).astype(jnp.bfloat16)  103 us
    all_gather x1, waiting for transfers between devices, per_device(): two_full = lax.all_gather(u_two, 'tiles', axis=1, tiled=True)  17.5 us
  transfers between devices with their start and end apart: 2, of which 2 were waited for; matrix products, arithmetic and copies ran while one was open for 1% of the time, Pallas kernels for 0%

profile of v1, /device:TPU:1, one launch (start us, length us, event | category | flops | bytes accessed | tf_op | source)
XLA Modules:
  0.0 853.6 jit_solution(17320908478926892155)
XLA Ops:
  7.2 0.0 all-gather.6.cloned.1.call-start
  7.2 0.7 all-gather.6.cloned.1.call-update
  7.9 0.0 reduce-scatter.4.cloned.1.call-start
  8.0 0.7 compare_select_fusion.3
  8.6 0.7 convert_bitcast_fusion.1
  9.3 1.0 reshape.51
  10.4 109.1 %all-gather.2 = bf16[128,64,32]{1,2,0:T(8,128)(2,1)S(1)} all-gather(bf16[1,64,32]{1,2,0:T(8,128)(2,1)S(1)} %convert_bitcast_fusion.1), channel_id=1, replica_groups=mesh['tiles'=128,'rep'=4] {'tiles'}, dimensions={0}, use_global_device_ids=true | all-gather | bytes 528384 | tf_op jit(solution)/shard_map/all_gather | solution.py:44
  119.5 0.4 copy.43
  119.9 0.8 reshape.105
  120.7 1.1 reshape.53
  121.9 0.7 copy.44
  122.6 3.4 reshape.52
  126.1 0.6 gather_fusion
  126.7 0.6 gather_fusion.2
  127.3 0.6 gather_fusion.3
  128.0 2.0 fusion
  130.0 17.5 %all-gather.6.cloned.1.call-done = bf16[32,16384]{1,0:T(8,128)(2,1)} async-done(((bf16[32,128]{1,0:T(8,128)(2,1)}), bf16[32,16384]{1,0:T(8,128)(2,1)}) %all-gather.6.cloned.1.call-update) | async-done | bytes 1048592 | tf_op jit(solution)/shard_map/all_gather | solution.py:54
  147.5 3.0 reshape.50
  150.6 2.7 copy.39
  153.3 2.1 gather_fusion.1
  155.4 1.1 fusion.1
  156.5 0.2 copy.42
  156.7 0.2 convolution_bitcast_fusion.1
  157.0 102.8 %all-reduce.1 = bf16[32,1024]{1,0:T(8,128)(2,1)S(1)} all-reduce(f32[32,1024]{1,0:T(8,128)S(1)} %convolution_bitcast_fusion.1), channel_id=1, replica_groups=mesh['tiles'=128,'rep'=4] {'tiles','rep'}, use_global_device_ids=true, to_apply=%region_0.0 | all-reduce | flops 32768 | bytes 196608 | tf_op jit(solution)/shard_map/psum | solution.py:70
  259.7 0.2 convolution_bitcast_fusion.2
  259.9 1.0 convolution_bitcast_fusion
  261.0 4.4 copy.57
  265.4 0.0 reduce-scatter.4.cloned.1.call-update
  265.5 245.9 %reduce-scatter.4.cloned.1.call-done = f32[64,32]{1,0:T(8,128)} async-done(((f32[8192,32]{1,0:T(8,128)}), f32[64,32]{1,0:T(8,128)}) %reduce-scatter.4.cloned.1.call-update) | async-done | bytes 8208
  511.3 0.8 copy.56
  512.2 13.3 %psum.15 = f32[32,64]{1,0:T(8,128)S(1)} all-reduce(f32[32,64]{1,0:T(8,128)S(1)} %copy.56), channel_id=1, replica_groups=mesh['tiles'=128,'rep'=4] {'rep'}, use_global_device_ids=true, to_apply=%region_2.4 | all-reduce | flops 2048 | bytes 16384 | tf_op jit(solution)/shard_map/psum | solution.py:74
  525.5 0.1 fusion.44
  525.6 115.5 %all-gather = f32[4096,32]{1,0:T(8,128)S(1)} all-gather(f32[32,32]{1,0:T(8,128)S(1)} %fusion.44), channel_id=2, replica_groups=mesh['tiles'=128,'rep'=4] {'tiles'}, dimensions={0}, use_global_device_ids=true | all-gather | bytes 528384 | tf_op jit(solution)/shard_map/all_gather | solution.py:10
  641.1 0.2 reduce_sum.28
  641.3 0.6 select_reduce_fusion
  642.6 0.1 fusion.6
  642.7 0.2 fusion.45
  642.9 99.5 %all-gather.1 = f32[4096,32]{1,0:T(8,128)S(1)} all-gather(f32[32,32]{1,0:T(8,128)S(1)} %fusion.45), channel_id=3, replica_groups=mesh['tiles'=128,'rep'=4] {'tiles'}, dimensions={0}, use_global_device_ids=true | all-gather | bytes 528384 | tf_op jit(solution)/shard_map/all_gather | solution.py:10
  742.4 0.2 reduce_sum.30
  742.6 0.1 fusion.7
  742.7 99.6 %all-gather.3 = bf16[128,64,32]{1,2,0:T(8,128)(2,1)S(1)} all-gather(bf16[1,64,32]{1,2,0:T(8,128)(2,1)S(1)} %convert_bitcast_fusion), channel_id=1, replica_groups=mesh['tiles'=128,'rep'=4] {'tiles'}, dimensions={0}, use_global_device_ids=true | all-gather | bytes 528384 | tf_op jit(solution)/shard_map/all_gather | solution.py:44
  842.4 0.4 copy.49
  842.8 0.8 reshape.107
  843.6 1.1 reshape.55
  844.7 0.7 copy.50
  845.4 0.6 gather_fusion.4
  846.0 0.1 broadcast_select_fusion
  846.1 0.7 reshape.56
  (22 shorter events, 0.1 us)
Async XLA Ops:
  7.2 118.9 %copy-start = (s32[128]{0:T(128)S(1)}, s32[128]{0:T(128)}, u32[]{:S(2)}) copy-start(s32[128]{0:T(128)} %param.14) | copy-start | bytes 1540
  7.2 140.3 %all-gather.6.cloned.1.call-start = ((), (), s32[]{:S(2)}) async-start(), calls=%async_computation.1 | async-start | bytes 1056768 | tf_op jit(solution)/shard_map/all_gather | solution.py:54
  7.9 503.4 %reduce-scatter.4.cloned.1.call-start = ((), (), s32[]{:S(2)}) async-start(), calls=%async_computation.2 | async-start | bytes 4227072
  122.6 4.2 copy-start.4
  122.6 4.7 copy-start.2
  122.6 5.3 copy-start.3
  742.7 100.9 %copy-start.1 = (f32[32,64]{1,0:T(8,128)}, f32[32,64]{1,0:T(8,128)S(1)}, u32[]{:S(2)}) copy-start(f32[32,64]{1,0:T(8,128)S(1)} %fusion.7) | copy-start | bytes 24580
Sparse Core Ops, SparseCore 0:
  11.0 136.4 all-gather.5
  265.6 245.7 reduce-scatter.3
